TPU v7x, 32 devices: a whole 2x2x4 slice. The times are simulated.
32 devices in a mesh: gx: 4 (over y, core), gy: 8 (over z, x).
Axes of the slice: x: 2, y: 2, z: 4, core: 2. Of those that a mesh axis runs over, the one named last changes fastest.
Arguments:
- density: float32 [80, 80, 384], P('gx', 'gy'), may hold values from 1e-06 to 0.5
- charge: float32 [80, 80, 384], P('gx', 'gy'), may hold values from -6 to 6
Outputs:
- solution_field: float32 [80, 80, 384], P('gx', 'gy')
- residual: float32 [80, 80, 384], P('gx', 'gy')
All inputs are finite; a program needn't handle non-finite values.
Results may differ from a plain program's by a relative error of at most 0.0003.
Values sent between devices are 32-bit elements; how exact they have to be, the bound alone decides.
No kernel may reach another device: no remote copies, remote signals or barrier semaphores. Data moves between devices by JAX's collectives and lax.ppermute only.
A program may use at most 64 MiB of HBM per device.

v0:
```python
import math
import jax
import jax.numpy as jnp
from jax import lax
from jax.sharding import PartitionSpec as P

EPS_SOLVENT = 78.3
RHO_UPPER = 0.005
RHO_LOWER = 0.0001
KAPPA_SCALE = 0.1
EPS_PRECOND = 20.0
SHIFT_PRECOND = 0.05
HIGHEST = lax.Precision.HIGHEST


def extended(block, sides, width):
    for axis, dim in sides:
        count = lax.axis_size(axis)
        forward = [(i, i + 1) for i in range(count - 1)]
        forward.append((count - 1, 0))
        backward = [(target, source) for source, target in forward]
        low = lax.ppermute(
            lax.slice_in_dim(block, block.shape[dim] - width, None, axis=dim), axis, forward
        )
        high = lax.ppermute(lax.slice_in_dim(block, 0, width, axis=dim), axis, backward)
        block = jnp.concatenate([low, block, high], axis=dim)
    return block


def permittivity(density):
    upper = math.log(RHO_UPPER)
    lower = math.log(RHO_LOWER)
    fraction = jnp.clip((upper - jnp.log(density)) / (upper - lower), 0.0, 1.0)
    exponent = fraction - jnp.sin(2.0 * math.pi * fraction) / (2.0 * math.pi)
    return jnp.exp(exponent * math.log(EPS_SOLVENT))


def hartley(length):
    indices = jnp.arange(length, dtype=jnp.int32)
    product = indices[:, None] * indices[None, :] % length
    angles = product.astype(jnp.float32) * (2.0 * math.pi / length)
    return jnp.cos(angles) + jnp.sin(angles)


def spectrum(wavenum, length):
    halfang = wavenum.astype(jnp.float32) * (math.pi / length)
    return ((27.0 * jnp.sin(halfang) - jnp.sin(3.0 * halfang)) / 12.0) ** 2


def cutout(values, offset, length, dimen):
    return lax.slice_in_dim(values, offset, offset + length, axis=dimen)


def padded_term(padded, faces, count, dimen):
    nfaces = count + 3
    grad = (
        27.0 * (cutout(padded, 2, nfaces, dimen) - cutout(padded, 1, nfaces, dimen))
        - (cutout(padded, 3, nfaces, dimen) - cutout(padded, 0, nfaces, dimen))
    ) / 24.0
    flux = faces * grad
    return (
        27.0 * (cutout(flux, 2, count, dimen) - cutout(flux, 1, count, dimen))
        - (cutout(flux, 3, count, dimen) - cutout(flux, 0, count, dimen))
    ) / 24.0


def rolled_term(field, faces):
    grad = (
        27.0 * (jnp.roll(field, -1, 2) - field) - (jnp.roll(field, -2, 2) - jnp.roll(field, 1, 2))
    ) / 24.0
    flux = faces * grad
    return (
        27.0 * (flux - jnp.roll(flux, 1, 2)) - (jnp.roll(flux, -1, 2) - jnp.roll(flux, 2, 2))
    ) / 24.0


def operate(field, faces_x, faces_y, faces_z, kappa):
    cellsx = field.shape[0]
    cellsy = field.shape[1]
    padded = extended(field, (("gx", 0), ("gy", 1)), 3)
    term_x = padded_term(padded[:, 3 : 3 + cellsy], faces_x, cellsx, 0)
    term_y = padded_term(padded[3 : 3 + cellsx], faces_y, cellsy, 1)
    term_z = rolled_term(field, faces_z)
    return kappa * field - (term_x + term_y + term_z)


def precondition(field):
    cellsx, cellsy, length_z = field.shape
    size_x = cellsx * lax.axis_size("gx")
    size_y = cellsy * lax.axis_size("gy")
    hart_x = hartley(size_x)
    hart_y = hartley(size_y)
    hart_z = hartley(length_z)
    scaling = float(size_x * size_y * length_z)
    forward = jnp.dot(field, hart_z, precision=HIGHEST)
    zpiece = length_z // lax.axis_size("gx")
    xpiece = size_x // lax.axis_size("gy")
    lines_x = lax.all_to_all(forward, "gx", split_axis=2, concat_axis=0, tiled=True)
    along_x = jnp.einsum("xyk,xa->yka", lines_x, hart_x, precision=HIGHEST)
    lines_y = lax.all_to_all(along_x, "gy", split_axis=2, concat_axis=0, tiled=True)
    along_y = jnp.einsum("ykb,yc->kbc", lines_y, hart_y, precision=HIGHEST)
    wave_z = lax.axis_index("gx") * zpiece + jnp.arange(zpiece, dtype=jnp.int32)
    wave_x = lax.axis_index("gy") * xpiece + jnp.arange(xpiece, dtype=jnp.int32)
    wave_y = jnp.arange(size_y, dtype=jnp.int32)
    symbol = (
        EPS_PRECOND
        * (
            spectrum(wave_z, length_z)[:, None, None]
            + spectrum(wave_x, size_x)[None, :, None]
            + spectrum(wave_y, size_y)[None, None, :]
        )
        + SHIFT_PRECOND
    )
    scaled = along_y / (symbol * scaling)
    back_y = jnp.einsum("kbc,cy->ykb", scaled, hart_y, precision=HIGHEST)
    lines_back = lax.all_to_all(back_y, "gy", split_axis=0, concat_axis=2, tiled=True)
    back_x = jnp.einsum("yka,ax->xyk", lines_back, hart_x, precision=HIGHEST)
    bricks = lax.all_to_all(back_x, "gx", split_axis=0, concat_axis=2, tiled=True)
    return jnp.dot(bricks, hart_z, precision=HIGHEST)


def residual_inner(residual, precond):
    return lax.psum(jnp.sum(residual * precond), ("gx", "gy"))


def local(density, charge):
    eps = permittivity(density)
    kappa = KAPPA_SCALE * (eps - 1.0) / (EPS_SOLVENT - 1.0)
    cellsx = eps.shape[0]
    cellsy = eps.shape[1]
    eps_padded = extended(eps, (("gx", 0), ("gy", 1)), 2)
    strip_x = eps_padded[:, 2 : 2 + cellsy]
    faces_x = 0.5 * (strip_x[:-1] + strip_x[1:])
    strip_y = eps_padded[2 : 2 + cellsx]
    faces_y = 0.5 * (strip_y[:, :-1] + strip_y[:, 1:])
    faces_z = 0.5 * (eps + jnp.roll(eps, -1, 2))
    rhs = 4.0 * math.pi * charge
    residual = rhs
    precond = precondition(residual)
    inner_now = residual_inner(residual, precond)
    image = operate(precond, faces_x, faces_y, faces_z, kappa)
    alpha = inner_now / lax.psum(jnp.sum(precond * image), ("gx", "gy"))
    solution_field = alpha * precond
    residual = residual - alpha * image
    return (solution_field, residual)


def solution(mesh):
    placed = (P("gx", "gy", None), P("gx", "gy", None))
    return jax.shard_map(
        local,
        mesh=mesh,
        in_specs=placed,
        out_specs=(P("gx", "gy", None), P("gx", "gy", None)),
        check_vma=False,
    )
```

profile of v0, /device:TPU:12, one launch (start us, length us, event | category | flops | bytes accessed | tf_op | source)
XLA Modules:
  0.0 139.1 jit_solution(10146124797497846084)
XLA Ops:
  0.6 4.3 %fusion.4 = f32[20,10,384]{2,0,1:T(8,128)S(1)} fusion(f32[20,10,384]{2,0,1:T(8,128)} %param.3), kind=kOutput, calls=%fused_computation.7 | convolution fusion | flops 355445760 | bytes 614400 | tf_op jit(solution)/shard_map/dot_general | solution.py:95
  4.9 1.4 %copy.11 = f32[20,10,384]{0,1,2:T(8,128)S(1)} copy(f32[20,10,384]{2,0,1:T(8,128)S(1)} %fusion.4) | data formatting | bytes 614400 | tf_op jit(solution)/shard_map/dot_general | solution.py:95
  6.3 1.9 %reshape.76 = f32[4,1,19200]{2,1,0:T(1,128)} reshape(f32[384,10,20]{2,1,0:T(8,128)S(1)} %bitcast.54) | data formatting | bytes 614400
  8.2 3.9 %all-to-all-start = ((f32[4,1,19200]{2,1,0:T(1,128)}), f32[4,1,19200]{2,1,0:T(1,128)S(1)}, u32[]{:S(2)}, u32[]{:S(2)}) async-start(f32[4,1,19200]{2,1,0:T(1,128)} %reshape.76), calls=%async_computation | async-start | bytes 614400 | tf_op jit(solution)/shard_map/all_to_all | solution.py:98
  12.1 4.9 %all-to-all-done = f32[4,1,19200]{2,1,0:T(1,128)S(1)} async-done(((f32[4,1,19200]{2,1,0:T(1,128)}), f32[4,1,19200]{2,1,0:T(1,128)S(1)}, u32[]{:S(2)}, u32[]{:S(2)}) %all-to-all-start) | async-done | bytes 307232 | tf_op jit(solution)/shard_map/all_to_all | solution.py:98
  17.0 0.5 broadcast.171
  17.5 1.5 %reduce = f32[4,19200]{1,0:T(4,128)S(1)} reduce(f32[4,1,19200]{2,1,0:T(1,128)S(1)} %all-to-all-done, f32[]{:T(128)} %broadcast.171), dimensions={1}, to_apply=%all_to_all.52.reduce_sub_computation | reduce | bytes 614404 | tf_op jit(solution)/shard_map/all_to_all | solution.py:98
  19.0 1.2 reshape.77
  20.3 1.9 %copy.12 = f32[20,10,4,96]{3,0,2,1:T(8,128)} copy(f32[20,10,4,96]{0,1,3,2:T(8,128)S(1)} %bitcast.53) | data formatting | bytes 614400 | tf_op jit(solution)/shard_map/all_to_all | solution.py:98
  22.2 1.1 all_to_all.55
  23.2 0.7 fusion.50
  23.9 0.1 copy.31
  24.1 1.3 reshape.78
  25.4 6.3 %all-to-all-start.1 = ((f32[8,1,9600]{2,1,0:T(1,128)}), f32[8,1,9600]{2,1,0:T(1,128)S(1)}, u32[]{:S(2)}, u32[]{:S(2)}) async-start(f32[8,1,9600]{2,1,0:T(1,128)} %reshape.78), calls=%async_computation.1 | async-start | bytes 614400 | tf_op jit(solution)/shard_map/all_to_all | solution.py:100
  31.8 0.1 broadcast_add_fusion
  31.9 8.7 %all-to-all-done.1 = f32[8,1,9600]{2,1,0:T(1,128)S(1)} async-done(((f32[8,1,9600]{2,1,0:T(1,128)}), f32[8,1,9600]{2,1,0:T(1,128)S(1)}, u32[]{:S(2)}, u32[]{:S(2)}) %all-to-all-start.1) | async-done | bytes 307232 | tf_op jit(solution)/shard_map/all_to_all | solution.py:100
  40.6 1.4 reduce.1
  41.9 0.3 reshape.79
  42.3 0.7 convolution_divide_fusion
  43.0 0.7 fusion.47
  43.7 0.1 copy.30
  43.9 1.3 reshape.80
  45.1 4.6 %all-to-all-start.2 = ((f32[8,1,9600]{2,1,0:T(1,128)}), f32[8,1,9600]{2,1,0:T(1,128)S(1)}, u32[]{:S(2)}, u32[]{:S(2)}) async-start(f32[8,1,9600]{2,1,0:T(1,128)} %reshape.80), calls=%async_computation.2 | async-start | bytes 614400 | tf_op jit(solution)/shard_map/all_to_all | solution.py:116
  49.7 1.3 multiply_exponential_fusion
  51.2 1.7 %collective-permute-start.1 = (f32[2,10,384]{2,0,1:T(2,128)S(1)}, f32[2,10,384]{2,0,1:T(2,128)S(1)}, u32[]{:S(2)}, u32[]{:S(2)}) collective-permute-start(f32[2,10,384]{2,0,1:T(2,128)S(1)} %get-tuple-element.12), channel_id=1, source_target_pairs={{8,0},{16,8},{24,16},{0,24},{9,1},{17,9},{25,17},{1,25},{10,2},{18... | collective-permute-start | bytes 92168 | tf_op jit(solution)/shard_map/ppermute | solution.py:25
  52.9 0.2 slice.204
  53.1 1.4 %collective-permute-done = f32[2,10,384]{2,0,1:T(2,128)S(1)} collective-permute-done((f32[2,10,384]{2,0,1:T(2,128)S(1)}, f32[2,10,384]{2,0,1:T(2,128)S(1)}, u32[]{:S(2)}, u32[]{:S(2)}) %collective-permute-start) | collective-permute-done | bytes 30752 | tf_op jit(solution)/shard_map/ppermute | solution.py:22
  54.5 1.5 %collective-permute-start.4 = (f32[24,2,384]{2,0,1:T(8,128)S(1)}, f32[24,2,384]{2,0,1:T(8,128)S(1)}, u32[]{:S(2)}, u32[]{:S(2)}) collective-permute-start(f32[24,2,384]{2,0,1:T(8,128)S(1)} %get-tuple-element.9), channel_id=1, source_target_pairs={{0,1},{1,2},{2,3},{3,4},{4,5},{5,6},{6,7},{7,0},{8,9},{9,10},{10,1... | collective-permute-start | bytes 221192 | tf_op jit(solution)/shard_map/ppermute | solution.py:22
  56.0 1.5 %collective-permute-start.5 = (f32[24,2,384]{2,0,1:T(8,128)S(1)}, f32[24,2,384]{2,0,1:T(8,128)S(1)}, u32[]{:S(2)}, u32[]{:S(2)}) collective-permute-start(f32[24,2,384]{2,0,1:T(8,128)S(1)} %get-tuple-element.10), channel_id=1, source_target_pairs={{1,0},{2,1},{3,2},{4,3},{5,4},{6,5},{7,6},{0,7},{9,8},{10,9},{11,1... | collective-permute-start | bytes 221192 | tf_op jit(solution)/shard_map/ppermute | solution.py:25
  57.5 0.7 all-to-all-done.2
  58.2 1.4 reduce.2
  59.6 0.3 reshape.81
  59.9 0.1 copy.18
  60.0 0.7 fusion.45
  60.7 0.1 copy.19
  60.9 1.3 reshape.82
  62.1 4.8 %all-to-all-start.3 = ((f32[4,1,19200]{2,1,0:T(1,128)}), f32[4,1,19200]{2,1,0:T(1,128)S(1)}, u32[]{:S(2)}, u32[]{:S(2)}) async-start(f32[4,1,19200]{2,1,0:T(1,128)} %reshape.82), calls=%async_computation.3 | async-start | bytes 614400 | tf_op jit(solution)/shard_map/all_to_all | solution.py:118
  67.0 0.1 pad_maximum_fusion.9
  67.0 0.1 pad_maximum_fusion.1
  67.1 4.7 %all-to-all-done.3 = f32[4,1,19200]{2,1,0:T(1,128)S(1)} async-done(((f32[4,1,19200]{2,1,0:T(1,128)}), f32[4,1,19200]{2,1,0:T(1,128)S(1)}, u32[]{:S(2)}, u32[]{:S(2)}) %all-to-all-start.3) | async-done | bytes 307232 | tf_op jit(solution)/shard_map/all_to_all | solution.py:118
  71.8 1.5 %reduce.3 = f32[4,19200]{1,0:T(4,128)S(1)} reduce(f32[4,1,19200]{2,1,0:T(1,128)S(1)} %all-to-all-done.3, f32[]{:T(128)} %broadcast.171), dimensions={1}, to_apply=%all_to_all.64.reduce_sub_computation | reduce | bytes 614404 | tf_op jit(solution)/shard_map/all_to_all | solution.py:118
  73.3 0.3 reshape.83
  73.6 0.3 copy.21
  73.9 0.2 all_to_all.67
  74.2 3.3 %fusion.2 = f32[20,10,384]{2,0,1:T(8,128)S(1)} fusion(f32[20,10,384]{2,0,1:T(8,128)S(1)} %all_to_all.67), kind=kOutput, calls=%fused_computation.5 | convolution fusion | flops 355368960 | bytes 614400 | tf_op jit(solution)/shard_map/dot_general | solution.py:119
  77.5 0.2 fusion.81
  77.6 0.1 fusion.80
  77.7 0.2 slice.208
  78.0 1.7 %collective-permute-start.3 = (f32[3,10,384]{2,0,1:T(4,128)S(1)}, f32[3,10,384]{2,0,1:T(4,128)S(1)}, u32[]{:S(2)}, u32[]{:S(2)}) collective-permute-start(f32[3,10,384]{2,0,1:T(4,128)S(1)} %get-tuple-element.14), channel_id=1, source_target_pairs={{8,0},{16,8},{24,16},{0,24},{9,1},{17,9},{25,17},{1,25},{10,2},{18... | collective-permute-start | bytes 138248 | tf_op jit(solution)/shard_map/ppermute | solution.py:25
  79.7 1.5 %fusion.29 = f32[20,10,384]{2,0,1:T(8,128)S(1)} fusion(f32[20,10,1]{2,0,1:T(8,128)S(1)} %slice-done, f32[20,10,383]{2,0,1:T(8,128)S(1)} %slice.204, f32[20,10,384]{2,0,1:T(8,128)S(1)} %fusion.2, f32[20,10,1]{2,0,1:T(8,128)S(1)} %get-tuple-element.20, f32[20,10,383]{2,0,1:T(8,128)S(1)} %get-tuple-element.22, f32[20,10,2]{2,0,1:T(8,128)S(1)} %slice.209, ...), kind=kLoop, calls=%fused_computation.53 | loop fusion | flops 1459200 | bytes 2150400 | tf_op jit(solution)/shard_map/mul | solution.py:71
  81.3 0.2 fusion.79
  81.4 0.1 fusion.78
  81.5 0.1 slice.216
  81.6 0.1 pad_maximum_fusion.2
  81.8 0.2 collective-permute-start.6
  82.0 2.7 %collective-permute-start.7 = (f32[26,3,384]{2,0,1:T(8,128)S(1)}, f32[26,3,384]{2,0,1:T(8,128)S(1)}, u32[]{:S(2)}, u32[]{:S(2)}) collective-permute-start(f32[26,3,384]{2,0,1:T(8,128)S(1)} %get-tuple-element.7), channel_id=1, source_target_pairs={{1,0},{2,1},{3,2},{4,3},{5,4},{6,5},{7,6},{0,7},{9,8},{10,9},{11,1... | collective-permute-start | bytes 359432 | tf_op jit(solution)/shard_map/ppermute | solution.py:25
  84.7 0.2 fusion.26
  85.0 3.8 %collective-permute-done.6 = f32[26,3,384]{2,0,1:T(8,128)S(1)} collective-permute-done((f32[26,3,384]{2,0,1:T(8,128)S(1)}, f32[26,3,384]{2,0,1:T(8,128)S(1)}, u32[]{:S(2)}, u32[]{:S(2)}) %collective-permute-start.6) | collective-permute-done | bytes 119840 | tf_op jit(solution)/shard_map/ppermute | solution.py:22
  88.8 2.7 %collective-permute-done.7 = f32[26,3,384]{2,0,1:T(8,128)S(1)} collective-permute-done((f32[26,3,384]{2,0,1:T(8,128)S(1)}, f32[26,3,384]{2,0,1:T(8,128)S(1)}, u32[]{:S(2)}, u32[]{:S(2)}) %collective-permute-start.7) | collective-permute-done | bytes 119840 | tf_op jit(solution)/shard_map/ppermute | solution.py:25
  91.5 0.1 pad_maximum_fusion
  91.6 0.3 fusion.12
  91.9 2.5 %multiply_reduce_fusion = (f32[]{:T(128)}, f32[]{:T(128)}, f32[20,10,384]{2,0,1:T(8,128)S(1)}) fusion(f32[20,10,384]{2,0,1:T(8,128)S(1)} %fusion.2, f32[20,10,384]{2,0,1:T(8,128)S(1)} %copy-done.2, f32[20,10,382]{2,0,1:T(8,128)S(1)} %bitcast.52, f32[20,10,2]{2,0,1:T(8,128)S(1)} %slice.216, f32[20,10,1]{2,0,1:T(8,128)S(1)} %get-tuple-element.16, ...), kind=kLoop, calls=%fused_computation.64 | loop fusion | flops 2611198 | bytes 4915208 | tf_op jit(solution)/shard_map/reduce_sum | solution.py:142
  94.5 42.4 %all-reduce = (f32[]{:T(128)}, f32[]{:T(128)}) all-reduce(f32[]{:T(128)} %get-tuple-element.3, f32[]{:T(128)} %get-tuple-element.2), channel_id=1, replica_groups=mesh['gx'=4,'gy'=8] {'gx','gy'}, use_global_device_ids=true, to_apply=%region_1.2 | all-reduce | flops 2 | bytes 16 | tf_op jit(solution)/shard_map/psum | solution.py:123
  138.1 0.9 multiply_subtract_fusion
  (26 shorter events, 0.6 us)
Async XLA Ops:
  8.2 8.8 %all-to-all-start = ((f32[4,1,19200]{2,1,0:T(1,128)}), f32[4,1,19200]{2,1,0:T(1,128)S(1)}, u32[]{:S(2)}, u32[]{:S(2)}) async-start(f32[4,1,19200]{2,1,0:T(1,128)} %reshape.76), calls=%async_computation | async-start | bytes 614400 | tf_op jit(solution)/shard_map/all_to_all | solution.py:98
  25.4 15.2 %all-to-all-start.1 = ((f32[8,1,9600]{2,1,0:T(1,128)}), f32[8,1,9600]{2,1,0:T(1,128)S(1)}, u32[]{:S(2)}, u32[]{:S(2)}) async-start(f32[8,1,9600]{2,1,0:T(1,128)} %reshape.78), calls=%async_computation.1 | async-start | bytes 614400 | tf_op jit(solution)/shard_map/all_to_all | solution.py:100
  42.3 7.5 %copy-start.1 = (f32[20,10,384]{2,0,1:T(8,128)S(1)}, f32[20,10,384]{2,0,1:T(8,128)}, u32[]{:S(2)}) copy-start(f32[20,10,384]{2,0,1:T(8,128)} %param.2) | copy-start | bytes 921604
  45.1 13.1 %all-to-all-start.2 = ((f32[8,1,9600]{2,1,0:T(1,128)}), f32[8,1,9600]{2,1,0:T(1,128)S(1)}, u32[]{:S(2)}, u32[]{:S(2)}) async-start(f32[8,1,9600]{2,1,0:T(1,128)} %reshape.80), calls=%async_computation.2 | async-start | bytes 614400 | tf_op jit(solution)/shard_map/all_to_all | solution.py:116
  51.1 16.0 %copy-start = (f32[20,10,384]{2,0,1:T(8,128)}, f32[20,10,384]{2,0,1:T(8,128)S(1)}, u32[]{:S(2)}) copy-start(f32[20,10,384]{2,0,1:T(8,128)S(1)} %multiply_exponential_fusion) | copy-start | bytes 921604
  51.1 3.4 %collective-permute-start = (f32[2,10,384]{2,0,1:T(2,128)S(1)}, f32[2,10,384]{2,0,1:T(2,128)S(1)}, u32[]{:S(2)}, u32[]{:S(2)}) collective-permute-start(f32[2,10,384]{2,0,1:T(2,128)S(1)} %get-tuple-element.11), channel_id=1, source_target_pairs={{0,8},{8,16},{16,24},{24,0},{1,9},{9,17},{17,25},{25,1},{2,10},{10... | collective-permute-start | bytes 92168 | tf_op jit(solution)/shard_map/ppermute | solution.py:22
  51.2 3.3 %collective-permute-start.1 = (f32[2,10,384]{2,0,1:T(2,128)S(1)}, f32[2,10,384]{2,0,1:T(2,128)S(1)}, u32[]{:S(2)}, u32[]{:S(2)}) collective-permute-start(f32[2,10,384]{2,0,1:T(2,128)S(1)} %get-tuple-element.12), channel_id=1, source_target_pairs={{8,0},{16,8},{24,16},{0,24},{9,1},{17,9},{25,17},{1,25},{10,2},{18... | collective-permute-start | bytes 92168 | tf_op jit(solution)/shard_map/ppermute | solution.py:25
  54.5 12.5 %collective-permute-start.4 = (f32[24,2,384]{2,0,1:T(8,128)S(1)}, f32[24,2,384]{2,0,1:T(8,128)S(1)}, u32[]{:S(2)}, u32[]{:S(2)}) collective-permute-start(f32[24,2,384]{2,0,1:T(8,128)S(1)} %get-tuple-element.9), channel_id=1, source_target_pairs={{0,1},{1,2},{2,3},{3,4},{4,5},{5,6},{6,7},{7,0},{8,9},{9,10},{10,1... | collective-permute-start | bytes 221192 | tf_op jit(solution)/shard_map/ppermute | solution.py:22
  56.0 11.0 %collective-permute-start.5 = (f32[24,2,384]{2,0,1:T(8,128)S(1)}, f32[24,2,384]{2,0,1:T(8,128)S(1)}, u32[]{:S(2)}, u32[]{:S(2)}) collective-permute-start(f32[24,2,384]{2,0,1:T(8,128)S(1)} %get-tuple-element.10), channel_id=1, source_target_pairs={{1,0},{2,1},{3,2},{4,3},{5,4},{6,5},{7,6},{0,7},{9,8},{10,9},{11,1... | collective-permute-start | bytes 221192 | tf_op jit(solution)/shard_map/ppermute | solution.py:25
  62.1 9.7 %all-to-all-start.3 = ((f32[4,1,19200]{2,1,0:T(1,128)}), f32[4,1,19200]{2,1,0:T(1,128)S(1)}, u32[]{:S(2)}, u32[]{:S(2)}) async-start(f32[4,1,19200]{2,1,0:T(1,128)} %reshape.82), calls=%async_computation.3 | async-start | bytes 614400 | tf_op jit(solution)/shard_map/all_to_all | solution.py:118
  73.9 5.8 %slice-start = ((f32[20,10,384]{2,0,1:T(8,128)}), f32[20,10,1]{2,0,1:T(8,128)S(1)}, s32[]{:S(2)}) async-start(f32[20,10,384]{2,0,1:T(8,128)} %copy-done), calls=%async_computation.4 | async-start | bytes 245760 | tf_op jit(solution)/shard_map/jit(_roll_static)/slice | solution.py:136
  77.9 3.7 %collective-permute-start.2 = (f32[3,10,384]{2,0,1:T(4,128)S(1)}, f32[3,10,384]{2,0,1:T(4,128)S(1)}, u32[]{:S(2)}, u32[]{:S(2)}) collective-permute-start(f32[3,10,384]{2,0,1:T(4,128)S(1)} %get-tuple-element.13), channel_id=1, source_target_pairs={{0,8},{8,16},{16,24},{24,0},{1,9},{9,17},{17,25},{25,1},{2,10},{10... | collective-permute-start | bytes 138248 | tf_op jit(solution)/shard_map/ppermute | solution.py:22
  78.0 3.7 %collective-permute-start.3 = (f32[3,10,384]{2,0,1:T(4,128)S(1)}, f32[3,10,384]{2,0,1:T(4,128)S(1)}, u32[]{:S(2)}, u32[]{:S(2)}) collective-permute-start(f32[3,10,384]{2,0,1:T(4,128)S(1)} %get-tuple-element.14), channel_id=1, source_target_pairs={{8,0},{16,8},{24,16},{0,24},{9,1},{17,9},{25,17},{1,25},{10,2},{18... | collective-permute-start | bytes 138248 | tf_op jit(solution)/shard_map/ppermute | solution.py:25
  81.8 7.0 %collective-permute-start.6 = (f32[26,3,384]{2,0,1:T(8,128)S(1)}, f32[26,3,384]{2,0,1:T(8,128)S(1)}, u32[]{:S(2)}, u32[]{:S(2)}) collective-permute-start(f32[26,3,384]{2,0,1:T(8,128)S(1)} %get-tuple-element.8), channel_id=1, source_target_pairs={{0,1},{1,2},{2,3},{3,4},{4,5},{5,6},{6,7},{7,0},{8,9},{9,10},{10,1... | collective-permute-start | bytes 359432 | tf_op jit(solution)/shard_map/ppermute | solution.py:22
  82.0 9.9 %copy-start.2 = (f32[20,10,384]{2,0,1:T(8,128)S(1)}, f32[20,10,384]{2,0,1:T(8,128)}, u32[]{:S(2)}) copy-start(f32[20,10,384]{2,0,1:T(8,128)} %param.3) | copy-start | bytes 921604
  82.0 9.5 %collective-permute-start.7 = (f32[26,3,384]{2,0,1:T(8,128)S(1)}, f32[26,3,384]{2,0,1:T(8,128)S(1)}, u32[]{:S(2)}, u32[]{:S(2)}) collective-permute-start(f32[26,3,384]{2,0,1:T(8,128)S(1)} %get-tuple-element.7), channel_id=1, source_target_pairs={{1,0},{2,1},{3,2},{4,3},{5,4},{6,5},{7,6},{0,7},{9,8},{10,9},{11,1... | collective-permute-start | bytes 359432 | tf_op jit(solution)/shard_map/ppermute | solution.py:25
where the time goes:
time: 140 us; the launch traced here: 139 us
  blocking collectives  42.4 us (30%)
  starting transfers between devices  29.1 us (21%)
  waiting for transfers between devices  26.9 us (19%)
  local copies, waits for them, and re-layouts  14.9 us (11%)
  other arithmetic  13.1 us (9%)
  matrix products  10.3 us (7%)
  between operations  2.36 us (2%)
    psum x1, blocking collectives, residual_inner(): return lax.psum(jnp.sum(residual * precond), ('gx', 'gy'))  42.4 us
    all_to_all x1, waiting for transfers between devices, precondition(): lax.all_to_all(along_x, 'gy', split_axis=2, concat_axis=0, tiled=True)  8.69 us
    unnamed x14, local copies, waits for them, and re-layouts  7.8 us
    ppermute x4, starting transfers between devices, extended(): lax.ppermute(lax.slice_in_dim(block, 0, width, axis=dim), axis, backward)  7.67 us
    all_to_all x1, starting transfers between devices, precondition(): lax.all_to_all(along_x, 'gy', split_axis=2, concat_axis=0, tiled=True)  6.25 us
    ppermute x4, waiting for transfers between devices, extended(): lax.ppermute(lax.slice_in_dim(block, block.shape[dim] - width, None, axis...  5.22 us
    all_to_all x1, waiting for transfers between devices, precondition(): lax.all_to_all(forward, 'gx', split_axis=2, concat_axis=0, tiled=True)  4.86 us
    all_to_all x1, starting transfers between devices, precondition(): lax.all_to_all(back_x, 'gx', split_axis=0, concat_axis=2, tiled=True)  4.82 us
  transfers between devices with their start and end apart: 12, of which 7 were waited for; matrix products, arithmetic and copies ran while one was open for 6% of the time, Pallas kernels for 0%

commit v1 on v0

--- a/solution.py
+++ b/solution.py
@@ -95,7 +95,10 @@
     forward = jnp.dot(field, hart_z, precision=HIGHEST)
     zpiece = length_z // lax.axis_size("gx")
     xpiece = size_x // lax.axis_size("gy")
-    lines_x = lax.all_to_all(forward, "gx", split_axis=2, concat_axis=0, tiled=True)
+    lines_x = jnp.concatenate(
+        lax.all_to_all(jnp.stack(jnp.split(forward, lax.axis_size("gx"), axis=2)), "gx", 0, 0),
+        axis=0,
+    )
     along_x = jnp.einsum("xyk,xa->yka", lines_x, hart_x, precision=HIGHEST)
     lines_y = lax.all_to_all(along_x, "gy", split_axis=2, concat_axis=0, tiled=True)
     along_y = jnp.einsum("ykb,yc->kbc", lines_y, hart_y, precision=HIGHEST)

time: 140 us -> 134 us (0.957)
  local copies, waits for them, and re-layouts: 14.9 us -> 8.36 us
  waiting for transfers between devices: 26.9 us -> 28.7 us
    all_to_all x3 -> x1, local copies, waits for them, and re-layouts: 3.52 us -> 0.04 us  [precondition(): lax.all_to_all(jnp.stack(jnp.split(forward, lax.axis_size('gx'), axis=2))...]
    unnamed x14 -> x12, local copies, waits for them, and re-layouts: 7.8 us -> 5.41 us
    all_to_all x1, waiting for transfers between devices: 4.86 us -> 6.83 us  [precondition(): lax.all_to_all(jnp.stack(jnp.split(forward, lax.axis_size('gx'), axis=2))...]
    all_to_all x1 -> x0, other arithmetic: 1.49 us -> none  [precondition(): lax.all_to_all(forward, 'gx', split_axis=2, concat_axis=0, tiled=True)]
    dot_general x1 -> x0, local copies, waits for them, and re-layouts: 1.42 us -> none  [precondition(): forward = jnp.dot(field, hart_z, precision=HIGHEST)]
where the time goes in v1:
time: 134 us
  blocking collectives  42.5 us (32%)
  starting transfers between devices  29.3 us (22%)
  waiting for transfers between devices  28.7 us (21%)
  other arithmetic  12.4 us (9%)
  matrix products  10.3 us (8%)
  local copies, waits for them, and re-layouts  8.36 us (6%)
  between operations  2.35 us (2%)
    psum x1, blocking collectives, residual_inner(): return lax.psum(jnp.sum(residual * precond), ('gx', 'gy'))  42.5 us
    all_to_all x1, waiting for transfers between devices, precondition(): lax.all_to_all(along_x, 'gy', split_axis=2, concat_axis=0, tiled=True)  8.69 us
    ppermute x4, starting transfers between devices, extended(): lax.ppermute(lax.slice_in_dim(block, 0, width, axis=dim), axis, backward)  7.67 us
    all_to_all x1, waiting for transfers between devices, precondition(): lax.all_to_all(jnp.stack(jnp.split(forward, lax.axis_size('gx'), axis=2))...  6.83 us
    all_to_all x1, starting transfers between devices, precondition(): lax.all_to_all(along_x, 'gy', split_axis=2, concat_axis=0, tiled=True)  6.25 us
    unnamed x12, local copies, waits for them, and re-layouts  5.41 us
    ppermute x4, waiting for transfers between devices, extended(): lax.ppermute(lax.slice_in_dim(block, block.shape[dim] - width, None, axis...  5.22 us
    all_to_all x1, starting transfers between devices, precondition(): lax.all_to_all(back_x, 'gx', split_axis=0, concat_axis=2, tiled=True)  4.82 us
  transfers between devices with their start and end apart: 12, of which 7 were waited for; matrix products, arithmetic and copies ran while one was open for 6% of the time, Pallas kernels for 0%

profile of v1, /device:TPU:12, one launch (start us, length us, event | category | flops | bytes accessed | tf_op | source)
XLA Modules:
  0.0 133.9 jit_solution(2906068588231922249)
XLA Ops:
  0.6 4.3 %fusion.4 = f32[20,10,384]{2,0,1:T(8,128)S(1)} fusion(f32[20,10,384]{2,0,1:T(8,128)} %param.3), kind=kOutput, calls=%fused_computation.7 | convolution fusion | flops 355445760 | bytes 614400 | tf_op jit(solution)/shard_map/dot_general | solution.py:95
  4.9 0.2 slice_bitcast_fusion.3
  5.1 0.8 pad_maximum_fusion.2
  5.9 3.9 %all-to-all-start = ((f32[4,20,10,96]{3,1,2,0:T(8,128)}), f32[4,20,10,96]{3,1,2,0:T(8,128)S(1)}, u32[]{:S(2)}, u32[]{:S(2)}) async-start(f32[4,20,10,96]{3,1,2,0:T(8,128)} %pad_maximum_fusion.2), calls=%async_computation | async-start | bytes 983040 | tf_op jit(solution)/shard_map/all_to_all | solution.py:99
  9.8 6.8 %all-to-all-done = f32[4,20,10,96]{3,1,2,0:T(8,128)S(1)} async-done(((f32[4,20,10,96]{3,1,2,0:T(8,128)}), f32[4,20,10,96]{3,1,2,0:T(8,128)S(1)}, u32[]{:S(2)}, u32[]{:S(2)}) %all-to-all-start) | async-done | bytes 307232 | tf_op jit(solution)/shard_map/all_to_all | solution.py:99
  16.7 0.7 fusion.50
  17.4 0.1 copy.29
  17.6 1.3 reshape.80
  18.9 6.3 %all-to-all-start.1 = ((f32[8,1,9600]{2,1,0:T(1,128)}), f32[8,1,9600]{2,1,0:T(1,128)S(1)}, u32[]{:S(2)}, u32[]{:S(2)}) async-start(f32[8,1,9600]{2,1,0:T(1,128)} %reshape.80), calls=%async_computation.1 | async-start | bytes 614400 | tf_op jit(solution)/shard_map/all_to_all | solution.py:103
  25.2 0.1 multiply_multiply_fusion.1
  25.3 0.1 broadcast_add_fusion
  25.4 8.7 %all-to-all-done.1 = f32[8,1,9600]{2,1,0:T(1,128)S(1)} async-done(((f32[8,1,9600]{2,1,0:T(1,128)}), f32[8,1,9600]{2,1,0:T(1,128)S(1)}, u32[]{:S(2)}, u32[]{:S(2)}) %all-to-all-start.1) | async-done | bytes 307232 | tf_op jit(solution)/shard_map/all_to_all | solution.py:103
  34.1 0.6 broadcast.171
  34.6 1.3 %reduce = f32[8,9600]{1,0:T(8,128)S(1)} reduce(f32[8,1,9600]{2,1,0:T(1,128)S(1)} %all-to-all-done.1, f32[]{:T(128)} %broadcast.171), dimensions={1}, to_apply=%all_to_all.43.reduce_sub_computation | reduce | bytes 614404 | tf_op jit(solution)/shard_map/all_to_all | solution.py:103
  36.0 0.3 reshape.81
  36.3 0.1 copy.13
  36.4 0.7 convolution_divide_fusion
  37.1 0.7 fusion.47
  37.8 0.1 copy.28
  37.9 1.3 reshape.82
  39.2 4.7 %all-to-all-start.2 = ((f32[8,1,9600]{2,1,0:T(1,128)}), f32[8,1,9600]{2,1,0:T(1,128)S(1)}, u32[]{:S(2)}, u32[]{:S(2)}) async-start(f32[8,1,9600]{2,1,0:T(1,128)} %reshape.82), calls=%async_computation.2 | async-start | bytes 614400 | tf_op jit(solution)/shard_map/all_to_all | solution.py:119
  43.9 1.3 multiply_exponential_fusion
  45.3 0.1 collective-permute-start
  45.4 1.7 %collective-permute-start.1 = (f32[2,10,384]{2,0,1:T(2,128)S(1)}, f32[2,10,384]{2,0,1:T(2,128)S(1)}, u32[]{:S(2)}, u32[]{:S(2)}) collective-permute-start(f32[2,10,384]{2,0,1:T(2,128)S(1)} %get-tuple-element.12), channel_id=1, source_target_pairs={{8,0},{16,8},{24,16},{0,24},{9,1},{17,9},{25,17},{1,25},{10,2},{18... | collective-permute-start | bytes 92168 | tf_op jit(solution)/shard_map/ppermute | solution.py:25
  47.1 0.2 slice.204
  47.3 1.4 %collective-permute-done = f32[2,10,384]{2,0,1:T(2,128)S(1)} collective-permute-done((f32[2,10,384]{2,0,1:T(2,128)S(1)}, f32[2,10,384]{2,0,1:T(2,128)S(1)}, u32[]{:S(2)}, u32[]{:S(2)}) %collective-permute-start) | collective-permute-done | bytes 30752 | tf_op jit(solution)/shard_map/ppermute | solution.py:22
  48.7 1.5 %collective-permute-start.4 = (f32[24,2,384]{2,0,1:T(8,128)S(1)}, f32[24,2,384]{2,0,1:T(8,128)S(1)}, u32[]{:S(2)}, u32[]{:S(2)}) collective-permute-start(f32[24,2,384]{2,0,1:T(8,128)S(1)} %get-tuple-element.9), channel_id=1, source_target_pairs={{0,1},{1,2},{2,3},{3,4},{4,5},{5,6},{6,7},{7,0},{8,9},{9,10},{10,1... | collective-permute-start | bytes 221192 | tf_op jit(solution)/shard_map/ppermute | solution.py:22
  50.2 1.5 %collective-permute-start.5 = (f32[24,2,384]{2,0,1:T(8,128)S(1)}, f32[24,2,384]{2,0,1:T(8,128)S(1)}, u32[]{:S(2)}, u32[]{:S(2)}) collective-permute-start(f32[24,2,384]{2,0,1:T(8,128)S(1)} %get-tuple-element.10), channel_id=1, source_target_pairs={{1,0},{2,1},{3,2},{4,3},{5,4},{6,5},{7,6},{0,7},{9,8},{10,9},{11,1... | collective-permute-start | bytes 221192 | tf_op jit(solution)/shard_map/ppermute | solution.py:25
  51.7 0.7 all-to-all-done.2
  52.4 1.4 %reduce.1 = f32[8,9600]{1,0:T(8,128)S(1)} reduce(f32[8,1,9600]{2,1,0:T(1,128)S(1)} %all-to-all-done.2, f32[]{:T(128)} %broadcast.171), dimensions={1}, to_apply=%all_to_all.47.reduce_sub_computation | reduce | bytes 614404 | tf_op jit(solution)/shard_map/all_to_all | solution.py:119
  53.8 0.3 reshape.83
  54.1 0.1 copy.16
  54.2 0.7 fusion.45
  54.9 0.1 copy.17
  55.0 1.3 reshape.84
  56.3 4.8 %all-to-all-start.3 = ((f32[4,1,19200]{2,1,0:T(1,128)}), f32[4,1,19200]{2,1,0:T(1,128)S(1)}, u32[]{:S(2)}, u32[]{:S(2)}) async-start(f32[4,1,19200]{2,1,0:T(1,128)} %reshape.84), calls=%async_computation.3 | async-start | bytes 614400 | tf_op jit(solution)/shard_map/all_to_all | solution.py:121
  61.1 0.1 pad_maximum_fusion.10
  61.2 0.1 pad_maximum_fusion.1
  61.3 4.7 %all-to-all-done.3 = f32[4,1,19200]{2,1,0:T(1,128)S(1)} async-done(((f32[4,1,19200]{2,1,0:T(1,128)}), f32[4,1,19200]{2,1,0:T(1,128)S(1)}, u32[]{:S(2)}, u32[]{:S(2)}) %all-to-all-start.3) | async-done | bytes 307232 | tf_op jit(solution)/shard_map/all_to_all | solution.py:121
  66.0 1.5 %reduce.2 = f32[4,19200]{1,0:T(4,128)S(1)} reduce(f32[4,1,19200]{2,1,0:T(1,128)S(1)} %all-to-all-done.3, f32[]{:T(128)} %broadcast.171), dimensions={1}, to_apply=%all_to_all.51.reduce_sub_computation | reduce | bytes 614404 | tf_op jit(solution)/shard_map/all_to_all | solution.py:121
  67.5 0.3 reshape.85
  67.8 0.3 copy.19
  68.1 0.2 all_to_all.54
  68.3 3.3 %fusion.2 = f32[20,10,384]{2,0,1:T(8,128)S(1)} fusion(f32[20,10,384]{2,0,1:T(8,128)S(1)} %all_to_all.54), kind=kOutput, calls=%fused_computation.5 | convolution fusion | flops 355368960 | bytes 614400 | tf_op jit(solution)/shard_map/dot_general | solution.py:122
  71.6 0.2 fusion.81
  71.8 0.1 fusion.80
  71.9 0.2 slice.208
  72.1 1.7 %collective-permute-start.3 = (f32[3,10,384]{2,0,1:T(4,128)S(1)}, f32[3,10,384]{2,0,1:T(4,128)S(1)}, u32[]{:S(2)}, u32[]{:S(2)}) collective-permute-start(f32[3,10,384]{2,0,1:T(4,128)S(1)} %get-tuple-element.14), channel_id=1, source_target_pairs={{8,0},{16,8},{24,16},{0,24},{9,1},{17,9},{25,17},{1,25},{10,2},{18... | collective-permute-start | bytes 138248 | tf_op jit(solution)/shard_map/ppermute | solution.py:25
  73.9 1.5 %fusion.29 = f32[20,10,384]{2,0,1:T(8,128)S(1)} fusion(f32[20,10,1]{2,0,1:T(8,128)S(1)} %slice-done, f32[20,10,383]{2,0,1:T(8,128)S(1)} %slice.204, f32[20,10,384]{2,0,1:T(8,128)S(1)} %fusion.2, f32[20,10,1]{2,0,1:T(8,128)S(1)} %get-tuple-element.20, f32[20,10,383]{2,0,1:T(8,128)S(1)} %get-tuple-element.22, f32[20,10,2]{2,0,1:T(8,128)S(1)} %slice.209, ...), kind=kLoop, calls=%fused_computation.54 | loop fusion | flops 1459200 | bytes 2150400 | tf_op jit(solution)/shard_map/mul | solution.py:71
  75.4 0.2 fusion.79
  75.6 0.1 fusion.78
  75.7 0.1 slice.216
  75.8 0.1 pad_maximum_fusion.3
  75.9 0.2 collective-permute-start.6
  76.2 2.7 %collective-permute-start.7 = (f32[26,3,384]{2,0,1:T(8,128)S(1)}, f32[26,3,384]{2,0,1:T(8,128)S(1)}, u32[]{:S(2)}, u32[]{:S(2)}) collective-permute-start(f32[26,3,384]{2,0,1:T(8,128)S(1)} %get-tuple-element.7), channel_id=1, source_target_pairs={{1,0},{2,1},{3,2},{4,3},{5,4},{6,5},{7,6},{0,7},{9,8},{10,9},{11,1... | collective-permute-start | bytes 359432 | tf_op jit(solution)/shard_map/ppermute | solution.py:25
  78.9 0.2 fusion.26
  79.1 3.8 %collective-permute-done.6 = f32[26,3,384]{2,0,1:T(8,128)S(1)} collective-permute-done((f32[26,3,384]{2,0,1:T(8,128)S(1)}, f32[26,3,384]{2,0,1:T(8,128)S(1)}, u32[]{:S(2)}, u32[]{:S(2)}) %collective-permute-start.6) | collective-permute-done | bytes 119840 | tf_op jit(solution)/shard_map/ppermute | solution.py:22
  82.9 2.5 %collective-permute-done.7 = f32[26,3,384]{2,0,1:T(8,128)S(1)} collective-permute-done((f32[26,3,384]{2,0,1:T(8,128)S(1)}, f32[26,3,384]{2,0,1:T(8,128)S(1)}, u32[]{:S(2)}, u32[]{:S(2)}) %collective-permute-start.7) | collective-permute-done | bytes 119840 | tf_op jit(solution)/shard_map/ppermute | solution.py:25
  85.5 0.1 pad_maximum_fusion
  85.6 0.3 fusion.12
  85.8 0.7 copy-done.2
  86.6 2.5 %multiply_reduce_fusion = (f32[]{:T(128)}, f32[]{:T(128)}, f32[20,10,384]{2,0,1:T(8,128)S(1)}) fusion(f32[20,10,384]{2,0,1:T(8,128)S(1)} %fusion.2, f32[20,10,384]{2,0,1:T(8,128)S(1)} %copy-done.2, f32[20,10,382]{2,0,1:T(8,128)S(1)} %bitcast.56, f32[20,10,2]{2,0,1:T(8,128)S(1)} %slice.216, f32[20,10,1]{2,0,1:T(8,128)S(1)} %get-tuple-element.16, ...), kind=kLoop, calls=%fused_computation.65 | loop fusion | flops 2611198 | bytes 4915208 | tf_op jit(solution)/shard_map/reduce_sum | solution.py:145
  89.1 42.5 %all-reduce = (f32[]{:T(128)}, f32[]{:T(128)}) all-reduce(f32[]{:T(128)} %get-tuple-element.3, f32[]{:T(128)} %get-tuple-element.2), channel_id=1, replica_groups=mesh['gx'=4,'gy'=8] {'gx','gy'}, use_global_device_ids=true, to_apply=%region_1.2 | all-reduce | flops 2 | bytes 16 | tf_op jit(solution)/shard_map/psum | solution.py:126
  132.9 0.9 multiply_subtract_fusion
  (24 shorter events, 0.5 us)
Async XLA Ops:
  5.9 10.8 %all-to-all-start = ((f32[4,20,10,96]{3,1,2,0:T(8,128)}), f32[4,20,10,96]{3,1,2,0:T(8,128)S(1)}, u32[]{:S(2)}, u32[]{:S(2)}) async-start(f32[4,20,10,96]{3,1,2,0:T(8,128)} %pad_maximum_fusion.2), calls=%async_computation | async-start | bytes 983040 | tf_op jit(solution)/shard_map/all_to_all | solution.py:99
  18.9 15.2 %all-to-all-start.1 = ((f32[8,1,9600]{2,1,0:T(1,128)}), f32[8,1,9600]{2,1,0:T(1,128)S(1)}, u32[]{:S(2)}, u32[]{:S(2)}) async-start(f32[8,1,9600]{2,1,0:T(1,128)} %reshape.80), calls=%async_computation.1 | async-start | bytes 614400 | tf_op jit(solution)/shard_map/all_to_all | solution.py:103
  39.2 4.7 %copy-start.1 = (f32[20,10,384]{2,0,1:T(8,128)S(1)}, f32[20,10,384]{2,0,1:T(8,128)}, u32[]{:S(2)}) copy-start(f32[20,10,384]{2,0,1:T(8,128)} %param.2) | copy-start | bytes 921604
  39.2 13.2 %all-to-all-start.2 = ((f32[8,1,9600]{2,1,0:T(1,128)}), f32[8,1,9600]{2,1,0:T(1,128)S(1)}, u32[]{:S(2)}, u32[]{:S(2)}) async-start(f32[8,1,9600]{2,1,0:T(1,128)} %reshape.82), calls=%async_computation.2 | async-start | bytes 614400 | tf_op jit(solution)/shard_map/all_to_all | solution.py:119
  45.3 16.0 %copy-start = (f32[20,10,384]{2,0,1:T(8,128)}, f32[20,10,384]{2,0,1:T(8,128)S(1)}, u32[]{:S(2)}) copy-start(f32[20,10,384]{2,0,1:T(8,128)S(1)} %multiply_exponential_fusion) | copy-start | bytes 921604
  45.3 3.4 %collective-permute-start = (f32[2,10,384]{2,0,1:T(2,128)S(1)}, f32[2,10,384]{2,0,1:T(2,128)S(1)}, u32[]{:S(2)}, u32[]{:S(2)}) collective-permute-start(f32[2,10,384]{2,0,1:T(2,128)S(1)} %get-tuple-element.11), channel_id=1, source_target_pairs={{0,8},{8,16},{16,24},{24,0},{1,9},{9,17},{17,25},{25,1},{2,10},{10... | collective-permute-start | bytes 92168 | tf_op jit(solution)/shard_map/ppermute | solution.py:22
  45.4 3.3 %collective-permute-start.1 = (f32[2,10,384]{2,0,1:T(2,128)S(1)}, f32[2,10,384]{2,0,1:T(2,128)S(1)}, u32[]{:S(2)}, u32[]{:S(2)}) collective-permute-start(f32[2,10,384]{2,0,1:T(2,128)S(1)} %get-tuple-element.12), channel_id=1, source_target_pairs={{8,0},{16,8},{24,16},{0,24},{9,1},{17,9},{25,17},{1,25},{10,2},{18... | collective-permute-start | bytes 92168 | tf_op jit(solution)/shard_map/ppermute | solution.py:25
  48.7 12.5 %collective-permute-start.4 = (f32[24,2,384]{2,0,1:T(8,128)S(1)}, f32[24,2,384]{2,0,1:T(8,128)S(1)}, u32[]{:S(2)}, u32[]{:S(2)}) collective-permute-start(f32[24,2,384]{2,0,1:T(8,128)S(1)} %get-tuple-element.9), channel_id=1, source_target_pairs={{0,1},{1,2},{2,3},{3,4},{4,5},{5,6},{6,7},{7,0},{8,9},{9,10},{10,1... | collective-permute-start | bytes 221192 | tf_op jit(solution)/shard_map/ppermute | solution.py:22
  50.2 11.0 %collective-permute-start.5 = (f32[24,2,384]{2,0,1:T(8,128)S(1)}, f32[24,2,384]{2,0,1:T(8,128)S(1)}, u32[]{:S(2)}, u32[]{:S(2)}) collective-permute-start(f32[24,2,384]{2,0,1:T(8,128)S(1)} %get-tuple-element.10), channel_id=1, source_target_pairs={{1,0},{2,1},{3,2},{4,3},{5,4},{6,5},{7,6},{0,7},{9,8},{10,9},{11,1... | collective-permute-start | bytes 221192 | tf_op jit(solution)/shard_map/ppermute | solution.py:25
  56.3 9.7 %all-to-all-start.3 = ((f32[4,1,19200]{2,1,0:T(1,128)}), f32[4,1,19200]{2,1,0:T(1,128)S(1)}, u32[]{:S(2)}, u32[]{:S(2)}) async-start(f32[4,1,19200]{2,1,0:T(1,128)} %reshape.84), calls=%async_computation.3 | async-start | bytes 614400 | tf_op jit(solution)/shard_map/all_to_all | solution.py:121
  72.0 1.8 %slice-start = ((f32[20,10,384]{2,0,1:T(8,128)}), f32[20,10,1]{2,0,1:T(8,128)S(1)}, s32[]{:S(2)}) async-start(f32[20,10,384]{2,0,1:T(8,128)} %copy-done), calls=%async_computation.4 | async-start | bytes 245760 | tf_op jit(solution)/shard_map/jit(_roll_static)/slice | solution.py:139
  72.1 3.7 %collective-permute-start.2 = (f32[3,10,384]{2,0,1:T(4,128)S(1)}, f32[3,10,384]{2,0,1:T(4,128)S(1)}, u32[]{:S(2)}, u32[]{:S(2)}) collective-permute-start(f32[3,10,384]{2,0,1:T(4,128)S(1)} %get-tuple-element.13), channel_id=1, source_target_pairs={{0,8},{8,16},{16,24},{24,0},{1,9},{9,17},{17,25},{25,1},{2,10},{10... | collective-permute-start | bytes 138248 | tf_op jit(solution)/shard_map/ppermute | solution.py:22
  72.1 3.7 %collective-permute-start.3 = (f32[3,10,384]{2,0,1:T(4,128)S(1)}, f32[3,10,384]{2,0,1:T(4,128)S(1)}, u32[]{:S(2)}, u32[]{:S(2)}) collective-permute-start(f32[3,10,384]{2,0,1:T(4,128)S(1)} %get-tuple-element.14), channel_id=1, source_target_pairs={{8,0},{16,8},{24,16},{0,24},{9,1},{17,9},{25,17},{1,25},{10,2},{18... | collective-permute-start | bytes 138248 | tf_op jit(solution)/shard_map/ppermute | solution.py:25
  75.9 7.0 %collective-permute-start.6 = (f32[26,3,384]{2,0,1:T(8,128)S(1)}, f32[26,3,384]{2,0,1:T(8,128)S(1)}, u32[]{:S(2)}, u32[]{:S(2)}) collective-permute-start(f32[26,3,384]{2,0,1:T(8,128)S(1)} %get-tuple-element.8), channel_id=1, source_target_pairs={{0,1},{1,2},{2,3},{3,4},{4,5},{5,6},{6,7},{7,0},{8,9},{9,10},{10,1... | collective-permute-start | bytes 359432 | tf_op jit(solution)/shard_map/ppermute | solution.py:22
  76.2 9.3 %collective-permute-start.7 = (f32[26,3,384]{2,0,1:T(8,128)S(1)}, f32[26,3,384]{2,0,1:T(8,128)S(1)}, u32[]{:S(2)}, u32[]{:S(2)}) collective-permute-start(f32[26,3,384]{2,0,1:T(8,128)S(1)} %get-tuple-element.7), channel_id=1, source_target_pairs={{1,0},{2,1},{3,2},{4,3},{5,4},{6,5},{7,6},{0,7},{9,8},{10,9},{11,1... | collective-permute-start | bytes 359432 | tf_op jit(solution)/shard_map/ppermute | solution.py:25
  85.6 1.0 copy-start.2
